TPU v7x, 512 devices: a whole 4x4x16 slice. The times are simulated.
512 devices in a mesh: tm: 16 (over y, x_lo, core), expert: 32 (over x_hi, z).
Axes of the slice: x: 4 (x_hi: 2, x_lo: 2; x = x_hi * 2 + x_lo), y: 4, z: 16, core: 2. Of those that a mesh axis runs over, the one named last changes fastest.
Arguments:
- latents: bfloat16 [32, 2048, 1024], P('expert', 'tm'), may hold values from -16 to 16
- queries: bfloat16 [32, 2048, 1024], P('expert', 'tm'), may hold values from -6 to 6
- keys: bfloat16 [32, 2048, 1024], P('expert', 'tm'), may hold values from -6 to 6
- values: bfloat16 [32, 2048, 1024], P('expert', 'tm'), may hold values from -8 to 8
- inpaint_mask: int32 [32, 2048], P('expert', 'tm'), may hold values 0 or 1
- key_bias: bfloat16 [16], replicated, may hold values from -3 to 3
- out_weight: bfloat16 [1024, 1024], replicated, may hold values from -0.1875 to 0.1875
- modulation: float32 [32, 2, 1024], P('expert'), may hold values from -3 to 3
- branch_gates: float32 [32, 2, 1024], P('expert'), may hold values from 0.5 to 1.5
- expert_ids: int32 [32, 2048, 2], P('expert', 'tm'), may hold values from 0 to 31, as said below
- gate_values: float32 [32, 2048, 2], P('expert', 'tm'), may hold values from 0.2 to 1
- up_weight: bfloat16 [32, 1024, 1024], P('expert', None, 'tm'), may hold values from -0.1875 to 0.1875
- down_weight: bfloat16 [32, 1024, 1024], P('expert', 'tm'), may hold values from -0.1875 to 0.1875
Outputs:
- layer_out: bfloat16 [32, 2048, 1024], P('expert', 'tm')
Inputs may be any that keep to these rules, and one draw needn't show every extreme that they name: `expert_ids`: A token's two ids differ. Within each device's block of 128 positions of one clip, no id is named more than 16 times, and one id is named exactly 16 times; that id is the same for all clips at the same block position.
All inputs are finite; a program needn't handle non-finite values. No bound on the sum of `inpaint_mask` on one device may be relied on, other than what follows from the above.
Results may differ from a plain program's by a relative error of at most 0.01.
Values may be sent and summed in bfloat16 or wider, within the bound.
A program may use at most 128 MiB of HBM per device.

v0:
```python
import jax
import jax.numpy as jnp
from jax import lax
from jax.sharding import PartitionSpec as P

eps = 1e-06
block_rows = 512


def key_block(carried, query_first, key_rows, value_rows, offset_rows):
    running_max, running_sum, weighted = carried
    key_first = jnp.transpose(key_rows, (1, 0, 2))
    value_first = jnp.transpose(value_rows, (1, 0, 2))
    scores = jnp.einsum("hqd,hkd->hqk", query_first, key_first, preferred_element_type=jnp.float32)
    scores = scores + jnp.transpose(offset_rows.astype(jnp.float32))[:, None, :]
    new_max = jnp.maximum(running_max, jnp.max(scores, axis=2))
    factor = jnp.exp(running_max - new_max)
    unscaled = jnp.exp(scores - new_max[:, :, None])
    running_sum = running_sum * factor + jnp.sum(unscaled, axis=2)
    weighted = weighted * factor[:, :, None] + jnp.einsum(
        "hqk,hkd->hqd",
        unscaled.astype(jnp.bfloat16),
        value_first,
        preferred_element_type=jnp.float32,
    )
    return (new_max, running_sum, weighted)


def layer_norm(mixed, shift_row, scale_row):
    center = jnp.mean(mixed, axis=-1, keepdims=True)
    deviation = mixed - center
    variance = jnp.mean(deviation * deviation, axis=-1, keepdims=True)
    return deviation * lax.rsqrt(variance + eps) * (1.0 + scale_row) + shift_row


def on_device(
    latents,
    queries,
    keys,
    values,
    inpaint_mask,
    key_bias,
    out_weight,
    modulation,
    branch_gates,
    expert_ids,
    gate_values,
    up_weight,
    down_weight,
):
    tok_rows = latents.shape[1]
    model_width = latents.shape[2]
    head_count = key_bias.shape[0]
    head_width = model_width // head_count
    score_scale = head_width ** (-0.5)
    scaled_queries = queries[0] * jnp.asarray(score_scale, jnp.bfloat16)
    query_heads = scaled_queries.reshape(tok_rows, head_count, head_width)
    key_heads = keys[0].reshape(tok_rows, head_count, head_width)
    value_heads = values[0].reshape(tok_rows, head_count, head_width)
    offsets = jnp.where(
        inpaint_mask[0][:, None] == 1, key_bias[None, :], jnp.zeros((), jnp.bfloat16)
    )
    full_up, full_down = (
        lax.all_gather(up_weight, "tm", axis=2, tiled=True),
        lax.all_gather(down_weight, "tm", axis=1, tiled=True),
    )
    query_first = jnp.transpose(query_heads, (1, 0, 2))
    initial = (
        jnp.full((head_count, tok_rows), -1e30, jnp.float32),
        jnp.zeros((head_count, tok_rows), jnp.float32),
        jnp.zeros((head_count, tok_rows, head_width), jnp.float32),
    )
    carried = initial
    key_part = lax.all_gather(key_heads, "tm", axis=0, tiled=True)
    value_part = lax.all_gather(value_heads, "tm", axis=0, tiled=True)
    offset_part = lax.all_gather(offsets, "tm", axis=0, tiled=True)
    row_count = key_part.shape[0]
    for first_row in range(0, row_count, block_rows):
        last_row = min(row_count, first_row + block_rows)
        carried = key_block(
            carried,
            query_first,
            key_part[first_row:last_row],
            value_part[first_row:last_row],
            offset_part[first_row:last_row],
        )
    running_max, running_sum, weighted = carried
    attended = jnp.transpose(weighted / running_sum[:, :, None], (1, 0, 2)).astype(jnp.bfloat16)
    projected = jnp.dot(
        attended.reshape(tok_rows, model_width), out_weight, preferred_element_type=jnp.float32
    )
    mixed = latents[0].astype(jnp.float32) + branch_gates[0, 0][None, :] * projected
    normed = layer_norm(mixed, modulation[0, 0][None, :], modulation[0, 1][None, :]).astype(
        jnp.bfloat16
    )
    local_experts = up_weight.shape[0]
    source_count = lax.axis_size("expert")
    expert_count = local_experts * source_count
    capacity = 4 * tok_rows // expert_count
    choice_list = expert_ids[0].reshape(2 * tok_rows)
    hits = (choice_list[:, None] == jnp.arange(expert_count, dtype=jnp.int32)[None, :]).astype(
        jnp.int32
    )
    ranks = jnp.sum((jnp.cumsum(hits, axis=0) - 1) * hits, axis=1)
    target = ranks * expert_count + choice_list
    placing = (
        jnp.arange(capacity * expert_count, dtype=jnp.int32)[:, None] == target[None, :]
    ).astype(jnp.bfloat16)
    doubled = jnp.repeat(normed, 2, axis=0)
    slots = jnp.dot(placing, doubled, preferred_element_type=jnp.float32).astype(jnp.bfloat16)
    slots = slots.reshape(capacity, expert_count, model_width)
    arrived = lax.all_to_all(slots, "expert", split_axis=1, concat_axis=1, tiled=True)
    slot_count = arrived.shape[0]
    grouped = arrived.reshape(slot_count, source_count, local_experts, model_width)
    hidden = jax.nn.gelu(
        jnp.einsum("csed,edf->csef", grouped, full_up, preferred_element_type=jnp.float32),
        approximate=True,
    ).astype(jnp.bfloat16)
    produced = jnp.einsum(
        "csef,efd->csed", hidden, full_down, preferred_element_type=jnp.float32
    ).astype(jnp.bfloat16)
    produced = produced.reshape(slot_count, source_count * local_experts, model_width)
    returned = lax.all_to_all(produced, "expert", split_axis=1, concat_axis=1, tiled=True)
    picked = jnp.einsum(
        "sa,sd->ad",
        placing,
        returned.reshape(capacity * expert_count, model_width),
        preferred_element_type=jnp.float32,
    )
    picked = picked.reshape(tok_rows, 2, model_width)
    combined = jnp.sum(gate_values[0][:, :, None] * picked, axis=1)
    layer_out = (mixed + branch_gates[0, 1][None, :] * combined).astype(jnp.bfloat16)
    return layer_out[None]


def solution(mesh):
    placed = (
        P("expert", "tm", None),
        P("expert", "tm", None),
        P("expert", "tm", None),
        P("expert", "tm", None),
        P("expert", "tm"),
        P(),
        P(),
        P("expert", None, None),
        P("expert", None, None),
        P("expert", "tm", None),
        P("expert", "tm", None),
        P("expert", None, "tm"),
        P("expert", "tm", None),
    )
    return jax.shard_map(
        on_device, mesh=mesh, in_specs=placed, out_specs=P("expert", "tm", None), check_vma=False
    )
```

profile of v0, /device:TPU:40, one launch (start us, length us, event | category | flops | bytes accessed | tf_op | source)
XLA Modules:
  0.0 301.7 jit_solution(3586965806504751508)
XLA Ops:
  6.5 0.0 copy-start
  6.5 0.0 all-gather.5.cloned.1.call-start
  6.5 1.9 copy.27
  8.5 0.0 all-gather.5.cloned.1.call-update
  8.5 0.0 all-gather.7.cloned.1.call-start
  8.6 1.8 copy.28
  10.3 0.0 all-gather.7.cloned.1.call-update
  10.4 0.0 all-gather.11.cloned.1.call-start
  10.4 0.7 all-gather.11.cloned.1.call-update
  11.1 0.8 copy.29
  11.9 0.1 eq.75
  12.0 0.1 eq.71
  12.2 0.7 compare_bitcast_fusion
  12.8 0.7 broadcast_select_fusion
  13.6 17.8 %all_gather.16 = bf16[2048,16]{0,1:T(8,128)(2,1)S(1)} all-gather(bf16[128,16]{0,1:T(8,128)(2,1)S(1)} %broadcast_select_fusion), channel_id=1, replica_groups=mesh['tm'=16,'expert'=32] {'tm'}, dimensions={0}, use_global_device_ids=true | all-gather | bytes 69632 | tf_op jit(solution)/shard_map/all_gather | solution.py:76
  31.4 1.1 copy.26
  32.6 0.8 fusion.115
  33.4 0.8 slice_add_fusion
  34.2 0.6 reduce-window.6
  34.8 0.2 slice_reduce_fusion
  35.0 0.1 fusion.98
  35.1 30.9 %all-gather.5.cloned.1.call-done = bf16[2048,16,64]{0,2,1:T(8,128)(2,1)} async-done(((bf16[128,16,64]{0,2,1:T(8,128)(2,1)}), bf16[2048,16,64]{0,2,1:T(8,128)(2,1)}) %all-gather.5.cloned.1.call-update) | async-done | bytes 4194320 | tf_op jit(solution)/shard_map/all_gather | solution.py:74
  66.0 2.2 add_reduce_fusion
  68.2 0.3 copy-done.8
  68.5 0.8 add_reduce_fusion.1
  69.4 0.8 add_reduce_fusion.2
  70.2 0.9 add_reduce_fusion.3
  71.1 2.4 fusion
  73.5 0.0 copy-done.3
  73.5 0.5 copy-done.5
  73.9 0.0 copy-done.6
  73.9 2.4 fusion.4
  76.3 44.9 %all-gather.7.cloned.1.call-done = bf16[2048,16,64]{0,2,1:T(8,128)(2,1)} async-done(((bf16[128,16,64]{0,2,1:T(8,128)(2,1)}), bf16[2048,16,64]{0,2,1:T(8,128)(2,1)}) %all-gather.7.cloned.1.call-update) | async-done | bytes 4194320 | tf_op jit(solution)/shard_map/all_gather | solution.py:75
  121.3 3.6 %fusion.76 = f32[128,16,64]{0,2,1:T(8,128)S(1)} fusion(f32[16,128,512]{2,1,0:T(8,128)} %copy-done.5, f32[16,128]{1,0:T(8,128)S(1)} %get-tuple-element.21, f32[16,512]{1,0:T(8,128)S(1)} %get-tuple-element.14, bf16[2048,16,64]{0,2,1:T(8,128)(2,1)} %all-gather.7.cloned.1.call-done, f32[128,16]{0,1:T(8,128)S(1)} %get-tuple-element.15, ...), kind=kOutput, calls=%fused_computation.58 | convolution fusion | flops 137625600 | bytes 5824512 | tf_op jit(solution)/shard_map/hqk,hkd->hqd/dot_general | solution.py:20
  124.9 0.1 copy-done.4
  125.0 2.4 fusion.70
  127.4 0.0 copy-done.2
  127.5 2.4 fusion.64
  129.8 0.0 copy-start.9
  129.9 0.1 copy-done.7
  129.9 2.3 fusion.82
  132.2 0.0 copy-done
  132.2 0.6 fusion.116
  132.8 0.2 multiply_reduce_fusion
  133.0 0.2 add_convert_fusion.1
  133.2 0.3 broadcast_in_dim.36
  133.5 1.0 reshape.204
  134.4 1.5 convolution_convert_fusion
  135.9 1.6 copy.32
  137.5 15.0 %all-to-all-start = ((bf16[16,32,1024]{2,0,1:T(8,128)(2,1)}), bf16[16,32,1024]{2,0,1:T(8,128)(2,1)}, u32[]{:S(2)}, u32[]{:S(2)}) async-start(bf16[16,32,1024]{2,0,1:T(8,128)(2,1)} %copy.32), calls=%async_computation | async-start | bytes 2097152 | tf_op jit(solution)/shard_map/all_to_all | solution.py:112
  152.5 0.2 all-gather.9.cloned.1.call-start
  152.7 0.3 all-gather.9.cloned.1.call-update
  153.1 12.7 %all-gather.11.cloned.1.call-done = bf16[1,1024,1024]{2,1,0:T(8,128)(2,1)} async-done(((bf16[1,64,1024]{2,1,0:T(8,128)(2,1)}), bf16[1,1024,1024]{2,1,0:T(8,128)(2,1)}) %all-gather.11.cloned.1.call-update) | async-done | bytes 2097168 | tf_op jit(solution)/shard_map/all_gather | solution.py:65
  165.7 45.5 %all-gather.9.cloned.1.call-done = bf16[1,1024,1024]{1,2,0:T(8,128)(2,1)} async-done(((bf16[1,1024,64]{1,2,0:T(8,128)(2,1)}), bf16[1,1024,1024]{1,2,0:T(8,128)(2,1)}) %all-gather.9.cloned.1.call-update) | async-done | bytes 2097168 | tf_op jit(solution)/shard_map/all_gather | solution.py:64
  211.3 0.0 all-to-all-done
  211.3 6.2 %fusion.38 = bf16[16,32,1024]{2,1,0:T(8,128)(2,1)} fusion(bf16[1,1024,1024]{2,1,0:T(8,128)(2,1)} %all-gather.11.cloned.1.call-done, bf16[1,1024,1024]{1,2,0:T(8,128)(2,1)} %all-gather.9.cloned.1.call-done, bf16[16,32,1024]{2,0,1:T(8,128)(2,1)} %all-to-all-done), kind=kOutput, calls=%fused_computation.41 | convolution fusion | flops 2152726528 | bytes 6291456 | tf_op jit(solution)/shard_map/csef,efd->csed/dot_general | solution.py:119
  217.5 2.8 copy.35
  220.3 15.4 %all-to-all-start.1 = ((bf16[16,32,1024]{2,0,1:T(8,128)(2,1)}), bf16[16,32,1024]{2,0,1:T(8,128)(2,1)}, u32[]{:S(2)}, u32[]{:S(2)}) async-start(bf16[16,32,1024]{2,0,1:T(8,128)(2,1)} %copy.35), calls=%async_computation.1 | async-start | bytes 2097152 | tf_op jit(solution)/shard_map/all_to_all | solution.py:123
  235.7 0.1 iota_compare_fusion.1
  235.9 0.2 eq.81
  236.0 56.1 %all-to-all-done.1 = bf16[16,32,1024]{2,0,1:T(8,128)(2,1)} async-done(((bf16[16,32,1024]{2,0,1:T(8,128)(2,1)}), bf16[16,32,1024]{2,0,1:T(8,128)(2,1)}, u32[]{:S(2)}, u32[]{:S(2)}) %all-to-all-start.1) | async-done | bytes 1048608 | tf_op jit(solution)/shard_map/all_to_all | solution.py:123
  292.1 1.8 copy.36
  294.0 0.4 fusion.44
  294.4 0.8 fusion.95
  (22 shorter events, 0.2 us)
Async XLA Ops:
  6.5 125.7 %copy-start = (bf16[1024,1024]{1,0:T(8,128)(2,1)S(1)}, bf16[1024,1024]{1,0:T(8,128)(2,1)}, u32[]{:S(2)}) copy-start(bf16[1024,1024]{1,0:T(8,128)(2,1)} %param.19) | copy-start | bytes 6291460
  6.5 59.5 %all-gather.5.cloned.1.call-start = ((), (), s32[]{:S(2)}) async-start(), calls=%async_computation.2 | async-start | bytes 4456448 | tf_op jit(solution)/shard_map/all_gather | solution.py:74
  8.5 112.8 %all-gather.7.cloned.1.call-start = ((), (), s32[]{:S(2)}) async-start(), calls=%async_computation.3 | async-start | bytes 4456448 | tf_op jit(solution)/shard_map/all_gather | solution.py:75
  10.4 155.4 %all-gather.11.cloned.1.call-start = ((), (), s32[]{:S(2)}) async-start(), calls=%async_computation.5 | async-start | bytes 2228224 | tf_op jit(solution)/shard_map/all_gather | solution.py:65
  66.0 2.5 copy-start.8
  68.2 5.7 %copy-start.6 = (f32[16,128,512]{2,1,0:T(8,128)}, f32[16,128,512]{2,1,0:T(8,128)S(1)}, u32[]{:S(2)}) copy-start(f32[16,128,512]{2,1,0:T(8,128)S(1)} %get-tuple-element.23) | copy-start | bytes 12582916
  69.4 4.6 %copy-start.1 = (f32[16,128,512]{2,1,0:T(8,128)}, f32[16,128,512]{2,1,0:T(8,128)S(1)}, u32[]{:S(2)}) copy-start(f32[16,128,512]{2,1,0:T(8,128)S(1)} %get-tuple-element.25) | copy-start | bytes 12582916
  70.2 3.3 %copy-start.3 = (f32[16,128,512]{2,1,0:T(8,128)}, f32[16,128,512]{2,1,0:T(8,128)S(1)}, u32[]{:S(2)}) copy-start(f32[16,128,512]{2,1,0:T(8,128)S(1)} %get-tuple-element.27) | copy-start | bytes 12582916
  71.1 2.9 copy-start.5
  121.3 3.8 %copy-start.4 = (f32[16,128,512]{2,1,0:T(8,128)S(1)}, f32[16,128,512]{2,1,0:T(8,128)}, u32[]{:S(2)}) copy-start(f32[16,128,512]{2,1,0:T(8,128)} %copy-done.3) | copy-start | bytes 12582916
  124.9 2.5 copy-start.2
  127.4 2.5 copy-start.7
  129.8 2.4 copy-start.9
  137.5 73.8 %all-to-all-start = ((bf16[16,32,1024]{2,0,1:T(8,128)(2,1)}), bf16[16,32,1024]{2,0,1:T(8,128)(2,1)}, u32[]{:S(2)}, u32[]{:S(2)}) async-start(bf16[16,32,1024]{2,0,1:T(8,128)(2,1)} %copy.32), calls=%async_computation | async-start | bytes 2097152 | tf_op jit(solution)/shard_map/all_to_all | solution.py:112
  152.5 58.8 %all-gather.9.cloned.1.call-start = ((), (), s32[]{:S(2)}) async-start(), calls=%async_computation.4 | async-start | bytes 2228224 | tf_op jit(solution)/shard_map/all_gather | solution.py:64
  217.5 76.5 %copy-start.10 = (f32[1,128,2]{1,2,0:T(2,128)S(1)}, f32[1,128,2]{1,2,0:T(2,128)}, u32[]{:S(2)}) copy-start(f32[1,128,2]{1,2,0:T(2,128)} %param.23) | copy-start | bytes 3076
  220.3 71.9 %all-to-all-start.1 = ((bf16[16,32,1024]{2,0,1:T(8,128)(2,1)}), bf16[16,32,1024]{2,0,1:T(8,128)(2,1)}, u32[]{:S(2)}, u32[]{:S(2)}) async-start(bf16[16,32,1024]{2,0,1:T(8,128)(2,1)} %copy.35), calls=%async_computation.1 | async-start | bytes 2097152 | tf_op jit(solution)/shard_map/all_to_all | solution.py:123
Sparse Core Ops, SparseCore 0:
  9.4 56.5 all-gather.4
  68.1 53.1 all-gather.6
  123.4 42.2 all-gather.10
  167.7 43.5 all-gather.8
where the time goes:
time: 302 us
  waiting for transfers between devices  191 us (63%)
  starting transfers between devices  30.7 us (10%)
  matrix products  24.1 us (8%)
  blocking collectives  17.8 us (6%)
  local copies, waits for them, and re-layouts  15.5 us (5%)
  between operations  13.4 us (4%)
  other arithmetic  9.02 us (3%)
    all_to_all x1, waiting for transfers between devices, on_device(): lax.all_to_all(produced, 'expert', split_axis=1, concat_axis=1, tiled=True)  56.1 us
    all_gather x1, waiting for transfers between devices, on_device(): lax.all_gather(up_weight, 'tm', axis=2, tiled=True)  45.5 us
    all_gather x1, waiting for transfers between devices, on_device(): value_part = lax.all_gather(value_heads, 'tm', axis=0, tiled=True)  44.9 us
    all_gather x1, waiting for transfers between devices, on_device(): key_part = lax.all_gather(key_heads, 'tm', axis=0, tiled=True)  30.9 us
    all_gather x1, blocking collectives, on_device(): offset_part = lax.all_gather(offsets, 'tm', axis=0, tiled=True)  17.8 us
    all_to_all x1, starting transfers between devices, on_device(): lax.all_to_all(produced, 'expert', split_axis=1, concat_axis=1, tiled=True)  15.4 us
    all_to_all x1, starting transfers between devices, on_device(): lax.all_to_all(slots, 'expert', split_axis=1, concat_axis=1, tiled=True)  15 us
    all_gather x1, waiting for transfers between devices, on_device(): lax.all_gather(down_weight, 'tm', axis=1, tiled=True)  12.7 us
  transfers between devices with their start and end apart: 6, of which 5 were waited for; matrix products, arithmetic and copies ran while one was open for 11% of the time, Pallas kernels for 0%

commit v1 on v0

--- a/solution.py
+++ b/solution.py
@@ -71,8 +71,11 @@
         jnp.zeros((head_count, tok_rows, head_width), jnp.float32),
     )
     carried = initial
-    key_part = lax.all_gather(key_heads, "tm", axis=0, tiled=True)
-    value_part = lax.all_gather(value_heads, "tm", axis=0, tiled=True)
+    key_part, value_part = jnp.split(
+        lax.all_gather(jnp.concatenate([key_heads, value_heads], axis=1), "tm", axis=0, tiled=True),
+        [key_heads.shape[1]],
+        axis=1,
+    )
     offset_part = lax.all_gather(offsets, "tm", axis=0, tiled=True)
     row_count = key_part.shape[0]
     for first_row in range(0, row_count, block_rows):

time: 302 us -> 262 us (0.87)
  the two profiles are of different devices: /device:TPU:40 before, /device:TPU:32 now
where the time goes in v1:
time: 262 us; the launch traced here: 261 us
  waiting for transfers between devices  160 us (61%)
  starting transfers between devices  27 us (10%)
  blocking collectives  20.1 us (8%)
  matrix products  19.8 us (8%)
  between operations  13.4 us (5%)
  local copies, waits for them, and re-layouts  12.4 us (5%)
  other arithmetic  8.7 us (3%)
    all_to_all x1, waiting for transfers between devices, on_device(): lax.all_to_all(produced, 'expert', split_axis=1, concat_axis=1, tiled=True)  56.1 us
    all_gather x1, waiting for transfers between devices, on_device(): lax.all_gather(jnp.concatenate([key_heads, value_heads], axis=1), 'tm', a...  46.8 us
    all_gather x1, waiting for transfers between devices, on_device(): lax.all_gather(down_weight, 'tm', axis=1, tiled=True)  44.5 us
    all_gather x1, blocking collectives, on_device(): offset_part = lax.all_gather(offsets, 'tm', axis=0, tiled=True)  20.1 us
    all_to_all x1, starting transfers between devices, on_device(): lax.all_to_all(slots, 'expert', split_axis=1, concat_axis=1, tiled=True)  14.7 us
    all_to_all x1, starting transfers between devices, on_device(): lax.all_to_all(produced, 'expert', split_axis=1, concat_axis=1, tiled=True)  12.1 us
    all_gather x1, waiting for transfers between devices, on_device(): lax.all_gather(up_weight, 'tm', axis=2, tiled=True)  7.46 us
    dot_general x4, matrix products, key_block(): jnp.einsum('hqd,hkd->hqk', query_first, key_first, preferred_element_type...  6.46 us
  transfers between devices with their start and end apart: 5, of which 5 were waited for; matrix products, arithmetic and copies ran while one was open for 10% of the time, Pallas kernels for 0%

profile of v1, /device:TPU:32, one launch (start us, length us, event | category | flops | bytes accessed | tf_op | source)
XLA Modules:
  0.0 261.2 jit_solution(10881265606860514632)
XLA Ops:
  6.5 0.0 copy-start
  6.5 0.0 copy-start.3
  6.5 0.0 copy-start.4
  6.5 0.0 all-gather.4.cloned.1.call-start
  6.5 1.3 copy.27
  7.8 1.1 copy.28
  8.9 0.9 pad_maximum_fusion
  9.8 0.0 all-gather.4.cloned.1.call-update
  9.9 0.0 all-gather.6.cloned.1.call-start
  9.9 0.7 all-gather.6.cloned.1.call-update
  10.6 0.8 copy.29
  11.4 0.1 eq.75
  11.5 0.1 eq.71
  11.7 0.7 compare_bitcast_fusion
  12.3 0.7 broadcast_select_fusion
  13.1 20.1 %all_gather.13 = bf16[2048,16]{0,1:T(8,128)(2,1)S(1)} all-gather(bf16[128,16]{0,1:T(8,128)(2,1)S(1)} %broadcast_select_fusion), channel_id=1, replica_groups=mesh['tm'=16,'expert'=32] {'tm'}, dimensions={0}, use_global_device_ids=true | all-gather | bytes 69632 | tf_op jit(solution)/shard_map/all_gather | solution.py:79
  33.2 1.1 copy.26
  34.3 0.0 copy-done.3
  34.4 0.0 copy-done.4
  34.4 0.6 reduce-window.6
  35.0 0.2 slice_reduce_fusion
  35.2 0.1 fusion.98
  35.3 46.8 %all-gather.4.cloned.1.call-done = bf16[2048,32,64]{0,2,1:T(8,128)(2,1)} async-done(((bf16[128,32,64]{0,2,1:T(8,128)(2,1)}), bf16[2048,32,64]{0,2,1:T(8,128)(2,1)}) %all-gather.4.cloned.1.call-update) | async-done | bytes 8388624 | tf_op jit(solution)/shard_map/all_gather | solution.py:75
  82.2 0.0 copy-start.1
  82.2 2.2 add_reduce_fusion
  84.4 2.6 add_reduce_fusion.1
  87.0 0.0 copy-done.1
  87.0 0.8 add_reduce_fusion.2
  87.8 0.8 add_reduce_fusion.3
  88.7 2.2 fusion
  90.8 2.2 fusion.4
  93.0 1.2 fusion.76
  94.2 1.2 fusion.70
  95.5 1.2 fusion.64
  96.7 0.0 copy-start.2
  96.7 1.0 fusion.82
  97.7 0.0 copy-done
  97.7 0.0 copy-done.2
  97.7 0.6 fusion.116
  98.3 0.2 multiply_reduce_fusion
  98.5 0.2 add_convert_fusion.1
  98.7 0.3 broadcast_in_dim.36
  99.0 1.0 reshape.204
  100.0 1.5 convolution_convert_fusion
  101.5 1.6 copy.32
  103.0 14.7 %all-to-all-start = ((bf16[16,32,1024]{2,0,1:T(8,128)(2,1)}), bf16[16,32,1024]{2,0,1:T(8,128)(2,1)}, u32[]{:S(2)}, u32[]{:S(2)}) async-start(bf16[16,32,1024]{2,0,1:T(8,128)(2,1)} %copy.32), calls=%async_computation | async-start | bytes 2097152 | tf_op jit(solution)/shard_map/all_to_all | solution.py:115
  117.7 0.2 all-gather.8.cloned.1.call-start
  118.0 0.5 all-gather.8.cloned.1.call-update
  118.5 7.5 %all-gather.6.cloned.1.call-done = bf16[1,1024,1024]{1,2,0:T(8,128)(2,1)} async-done(((bf16[1,1024,64]{1,2,0:T(8,128)(2,1)}), bf16[1,1024,1024]{1,2,0:T(8,128)(2,1)}) %all-gather.6.cloned.1.call-update) | async-done | bytes 2097168 | tf_op jit(solution)/shard_map/all_gather | solution.py:64
  125.9 44.5 %all-gather.8.cloned.1.call-done = bf16[1,1024,1024]{2,1,0:T(8,128)(2,1)} async-done(((bf16[1,64,1024]{2,1,0:T(8,128)(2,1)}), bf16[1,1024,1024]{2,1,0:T(8,128)(2,1)}) %all-gather.8.cloned.1.call-update) | async-done | bytes 2097168 | tf_op jit(solution)/shard_map/all_gather | solution.py:65
  170.4 3.8 %all-to-all-done = bf16[16,32,1024]{2,0,1:T(8,128)(2,1)} async-done(((bf16[16,32,1024]{2,0,1:T(8,128)(2,1)}), bf16[16,32,1024]{2,0,1:T(8,128)(2,1)}, u32[]{:S(2)}, u32[]{:S(2)}) %all-to-all-start) | async-done | bytes 1048608 | tf_op jit(solution)/shard_map/all_to_all | solution.py:115
  174.2 6.2 %fusion.38 = bf16[16,32,1024]{2,1,0:T(8,128)(2,1)} fusion(bf16[1,1024,1024]{2,1,0:T(8,128)(2,1)} %all-gather.8.cloned.1.call-done, bf16[1,1024,1024]{1,2,0:T(8,128)(2,1)} %all-gather.6.cloned.1.call-done, bf16[16,32,1024]{2,0,1:T(8,128)(2,1)} %all-to-all-done), kind=kOutput, calls=%fused_computation.41 | convolution fusion | flops 2152726528 | bytes 6291456 | tf_op jit(solution)/shard_map/csef,efd->csed/dot_general | solution.py:122
  180.4 0.0 copy-start.5
  180.4 2.8 %copy.35 = bf16[16,32,1024]{2,0,1:T(8,128)(2,1)} copy(bf16[16,32,1024]{2,1,0:T(8,128)(2,1)} %fusion.38) | data formatting | bytes 2097152 | tf_op jit(solution)/shard_map/convert_element_type | solution.py:124
  183.2 12.1 %all-to-all-start.1 = ((bf16[16,32,1024]{2,0,1:T(8,128)(2,1)}), bf16[16,32,1024]{2,0,1:T(8,128)(2,1)}, u32[]{:S(2)}, u32[]{:S(2)}) async-start(bf16[16,32,1024]{2,0,1:T(8,128)(2,1)} %copy.35), calls=%async_computation.1 | async-start | bytes 2097152 | tf_op jit(solution)/shard_map/all_to_all | solution.py:126
  195.3 0.1 iota_compare_fusion.1
  195.4 0.2 eq.81
  195.6 56.1 %all-to-all-done.1 = bf16[16,32,1024]{2,0,1:T(8,128)(2,1)} async-done(((bf16[16,32,1024]{2,0,1:T(8,128)(2,1)}), bf16[16,32,1024]{2,0,1:T(8,128)(2,1)}, u32[]{:S(2)}, u32[]{:S(2)}) %all-to-all-start.1) | async-done | bytes 1048608 | tf_op jit(solution)/shard_map/all_to_all | solution.py:126
  251.7 1.8 copy.36
  253.5 0.0 copy-done.5
  253.5 0.4 fusion.44
  253.9 0.8 fusion.95
  (12 shorter events, 0.2 us)
Async XLA Ops:
  6.5 91.2 %copy-start = (bf16[1024,1024]{1,0:T(8,128)(2,1)S(1)}, bf16[1024,1024]{1,0:T(8,128)(2,1)}, u32[]{:S(2)}) copy-start(bf16[1024,1024]{1,0:T(8,128)(2,1)} %param.19) | copy-start | bytes 6291460
  6.5 27.8 %copy-start.3 = (f32[1,2,1024]{2,1,0:T(2,128)S(1)}, f32[1,2,1024]{2,1,0:T(2,128)}, u32[]{:S(2)}) copy-start(f32[1,2,1024]{2,1,0:T(2,128)} %param.21) | copy-start | bytes 24580
  6.5 27.8 %copy-start.4 = (f32[1,2,1024]{2,1,0:T(2,128)S(1)}, f32[1,2,1024]{2,1,0:T(2,128)}, u32[]{:S(2)}) copy-start(f32[1,2,1024]{2,1,0:T(2,128)} %param.20) | copy-start | bytes 24580
  6.5 75.6 %all-gather.4.cloned.1.call-start = ((), (), s32[]{:S(2)}) async-start(), calls=%async_computation.2 | async-start | bytes 8912896 | tf_op jit(solution)/shard_map/all_gather | solution.py:75
  9.9 116.1 %all-gather.6.cloned.1.call-start = ((), (), s32[]{:S(2)}) async-start(), calls=%async_computation.3 | async-start | bytes 2228224 | tf_op jit(solution)/shard_map/all_gather | solution.py:64
  82.2 4.8 %copy-start.1 = (bf16[2048,32,64]{0,2,1:T(8,128)(2,1)S(1)}, bf16[2048,32,64]{0,2,1:T(8,128)(2,1)}, u32[]{:S(2)}) copy-start(bf16[2048,32,64]{0,2,1:T(8,128)(2,1)} %all-gather.4.cloned.1.call-done) | copy-start | bytes 25165828
  96.7 1.0 copy-start.2
  103.0 71.2 %all-to-all-start = ((bf16[16,32,1024]{2,0,1:T(8,128)(2,1)}), bf16[16,32,1024]{2,0,1:T(8,128)(2,1)}, u32[]{:S(2)}, u32[]{:S(2)}) async-start(bf16[16,32,1024]{2,0,1:T(8,128)(2,1)} %copy.32), calls=%async_computation | async-start | bytes 2097152 | tf_op jit(solution)/shard_map/all_to_all | solution.py:115
  117.7 52.6 %all-gather.8.cloned.1.call-start = ((), (), s32[]{:S(2)}) async-start(), calls=%async_computation.4 | async-start | bytes 2228224 | tf_op jit(solution)/shard_map/all_gather | solution.py:65
  180.4 73.1 %copy-start.5 = (f32[1,128,2]{1,2,0:T(2,128)S(1)}, f32[1,128,2]{1,2,0:T(2,128)}, u32[]{:S(2)}) copy-start(f32[1,128,2]{1,2,0:T(2,128)} %param.23) | copy-start | bytes 3076
  183.2 68.5 %all-to-all-start.1 = ((bf16[16,32,1024]{2,0,1:T(8,128)(2,1)}), bf16[16,32,1024]{2,0,1:T(8,128)(2,1)}, u32[]{:S(2)}, u32[]{:S(2)}) async-start(bf16[16,32,1024]{2,0,1:T(8,128)(2,1)} %copy.35), calls=%async_computation.1 | async-start | bytes 2097152 | tf_op jit(solution)/shard_map/all_to_all | solution.py:126
Sparse Core Ops, SparseCore 0:
  10.0 72.1 all-gather.3
  84.3 41.5 all-gather.5
  128.1 42.2 all-gather.7
